TPU v7x, 768 devices: a whole 4x8x12 slice. The times are simulated.
768 devices in a mesh: dom: 24 (over y_hi, z), sub: 32 (over x, y_lo, core).
Axes of the slice: x: 4, y: 8 (y_hi: 2, y_lo: 4; y = y_hi * 4 + y_lo), z: 12, core: 2. Of those that a mesh axis runs over, the one named last changes fastest.
Arguments:
- coefficients: float32 [9, 56, 98304], P(None, None, ('dom', 'sub')), may hold values from -6 to 6
- stiffness: float32 [3, 56, 56], replicated, may hold values from -0.75 to 0.75
- jacobians: float32 [3, 9, 9, 98304], P(None, None, None, ('dom', 'sub')), may hold values from -1.25 to 1.25
- face_proj: float32 [4, 21, 56], replicated, may hold values from -0.75 to 0.75
- neigh_proj: float32 [12, 21, 56], replicated, may hold values from -0.75 to 0.75
- lifting: float32 [4, 56, 21], replicated, may hold values from -1.25 to 1.25
- flux_local: float32 [4, 9, 9, 98304], P(None, None, None, ('dom', 'sub')), may hold values from -2 to 2
- flux_neigh: float32 [4, 9, 9, 98304], P(None, None, None, ('dom', 'sub')), may hold values from -2 to 2
- clusters: int32 [98304], P(('dom', 'sub')), may hold values from 0 to 2
- face_slots: int32 [4, 98304], P(None, ('dom', 'sub')), may hold values from 0 to 192, as said below
- orientation: int32 [4, 98304], P(None, ('dom', 'sub')), may hold values from 0 to 11
- send_list: int32 [4, 12288], P(None, ('dom', 'sub')), may hold values from 0 to 127, as said below
Outputs:
- increment: float32 [9, 56, 98304], P(None, None, ('dom', 'sub'))
Inputs may be any that keep to these rules, and one draw needn't show every extreme that they name: `face_slots`: A face refers to another local element (entry below 128, never the element itself), to a received element, or to the last entry (no neighbour). Every received entry of a neighbour that exists is referred to by exactly one face of the partition; entries of neighbours that do not exist are never referred to. `send_list`: the 16 entries of one row of one partition are distinct local element numbers.
All inputs are finite; a program needn't handle non-finite values.
Results may differ from a plain program's by a relative error of at most 0.0003.
Values sent between devices are 32-bit elements; how exact they have to be, the bound alone decides.
A program may use at most 192 MiB of HBM per device.

v0:
```python
import math

import jax
import jax.numpy as jnp
from jax import lax
from jax.experimental import pallas as pl
from jax.experimental.pallas import tpu as pltpu
from jax.sharding import PartitionSpec as P

Q = 9
B = 56
C = 21
CP = 24
E = 128
R = 16
ORDER = 6
ORIENTS = 12
SUBSTEPS = 4
STEP_LENGTH = 0.5
F32 = jnp.float32
BF16 = jnp.bfloat16
MESH = pl.DeviceIdType.MESH
OPPOSITE = (1, 0, 3, 2)
NT = (((1,), (1,)), ((), ()))
HIGHEST = lax.Precision.HIGHEST


def iota(shape, dim):
    return lax.broadcasted_iota(jnp.int32, shape, dim)


def halves(x):
    hi = x.astype(BF16)
    return hi, (x - hi.astype(F32)).astype(BF16)


def mm(a, b):
    return jnp.dot(a, b, preferred_element_type=F32)


def exact(a, b):
    return jnp.dot(a, b, preferred_element_type=F32, precision=HIGHEST)


def onehot(cond):
    return jnp.where(cond, 1.0, 0.0).astype(BF16)


def kernel(
    coef, stiff, jac, fproj, nproj, lift, floc, fnei, clus, slots, orient, slist,
    out,
    wf, w_d, w_u, w_n, w_l, oh_loc, oh_rem, oh_send, or_rem,
    rhs, sp, own, upd, app, pend, wt, trn, tn, tl_hi, tl_lo, flux, rhs_l, rhs_r, tt,
    send, recv, send_sem, recv_sem,
):
    sub, dom = lax.axis_index("sub"), lax.axis_index("dom")
    subs, doms = lax.axis_size("sub"), lax.axis_size("dom")
    peers = ({"sub": sub - 1}, {"sub": sub + 1}, {"dom": dom - 1}, {"dom": dom + 1})
    has = (sub > 0, sub < subs - 1, dom > 0, dom < doms - 1)
    barrier = pltpu.get_barrier_semaphore()
    for r in range(4):
        @pl.when(has[r])
        def _():
            pl.semaphore_signal(barrier, inc=1, device_id=peers[r], device_id_type=MESH)

        @pl.when(jnp.logical_not(has[r]))
        def _():
            for j in range(SUBSTEPS):
                recv[j, r] = jnp.zeros((R, 512), F32)

    def copy(j, r, slot):
        return pltpu.make_async_remote_copy(
            src_ref=send.at[j, r],
            dst_ref=recv.at[j, slot],
            send_sem=send_sem.at[j, r],
            recv_sem=recv_sem.at[j, slot],
            device_id=peers[r],
            device_id_type=MESH,
        )

    def triple(rows, width, step, x):
        place = jnp.where(
            (iota((x.shape[1], width), 1) % step == iota((x.shape[1], width), 0))
            & (iota((x.shape[1], width), 1) < 3 * step), 1.0, 0.0)
        return exact(x, place)

    def pack(x, step):
        hi = x.astype(BF16).astype(F32)
        return jnp.where(iota(x.shape, 1) < 2 * step, hi, x - hi).astype(BF16)

    for d in range(3):
        wf[d * B:(d + 1) * B, :] = triple(B, 192, 64, stiff[d])
    w_d[...] = pack(wf[0:3 * B, :], 64)

    def prepare_send():
        rows = iota((64, R), 0)
        picked = slist[0:1, :]
        picked = jnp.where(rows // R == 0, slist[0:1, :], jnp.where(
            rows // R == 1, slist[1:2, :], jnp.where(
                rows // R == 2, slist[2:3, :], slist[3:4, :])))
        picked = jnp.where(rows % R == iota((64, R), 1), picked.astype(F32), 0.0)
        column = jnp.sum(picked, axis=1, keepdims=True)
        oh_send[...] = onehot(iota((64, E), 1).astype(F32) == column)

    def prepare_rest():
        eye = jnp.where(iota((B, B), 0) == iota((B, B), 1), 1.0, 0.0)
        for d in range(3):
            turned = lax.dot_general(eye, stiff[d], NT, precision=HIGHEST, preferred_element_type=F32)
            wf[d * B:(d + 1) * B, :] = triple(B, 192, 64, turned)
        zero = jnp.zeros((CP - C, 192), F32)
        for f in range(4):
            wf[3 * B + f * CP:3 * B + (f + 1) * CP, :] = jnp.concatenate(
                [triple(C, 192, 64, fproj[:, f, :]), zero], axis=0)
        w_u[...] = pack(wf[0:3 * B + 4 * CP, :], 64)
        for o in range(ORIENTS):
            wf[o * CP:(o + 1) * CP, :] = jnp.concatenate(
                [triple(C, 192, 64, nproj[o]), zero], axis=0)
        w_n[...] = pack(wf[...], 64)
        total = None
        for f in range(4):
            spot = iota((C, 288), 1)
            place = jnp.where(spot % 96 == iota((C, 288), 0) + f * CP, 1.0, 0.0)
            turned = lax.dot_general(eye, lift[:, f, :], NT, precision=HIGHEST, preferred_element_type=F32)
            part = exact(turned, place)
            total = part if total is None else total + part
        w_l[...] = pack(total, 96)
        for f in range(4):
            cols = slice(f * E, (f + 1) * E)
            row = jnp.broadcast_to(slots[f:f + 1, :], (E, E))
            pair = jnp.broadcast_to(orient[f:f + 1, :], (E, E))
            here = onehot(iota((E, E), 0) == row)
            for o in range(ORIENTS):
                oh_loc[o * E:(o + 1) * E, cols] = here * onehot(pair == o)
            entry = iota((E, E), 0)
            first = onehot(entry + E == row) * onehot(entry < 64)
            second = onehot(entry + 64 == row) * onehot(entry >= 64)
            for k in range(2):
                oh_rem[k * E:(k + 1) * E, f * E:(f + 1) * E] = first
                oh_rem[k * E:(k + 1) * E, 512 + f * E:512 + (f + 1) * E] = second
        total = None
        for f in range(4):
            row = jnp.broadcast_to(orient[f:f + 1, :].astype(F32), (8, E)).astype(BF16)
            both = oh_rem[0:E, f * E:(f + 1) * E] + oh_rem[0:E, 512 + f * E:512 + (f + 1) * E]
            part = lax.dot_general(row, both, NT, preferred_element_type=F32)
            total = part if total is None else total + part
        or_rem[...] = total

    prepare_send()
    app[...] = jnp.zeros((Q, B, E), F32)
    pend[...] = jnp.zeros((Q, B, E), F32)

    def split_store(x, q):
        hi, lo = halves(jnp.concatenate([x, jnp.zeros((64 - B, E), F32)], axis=0))
        cols = pl.ds(q * E if isinstance(q, int) else pl.multiple_of(q * E, E), E)
        rhs[0:64, cols] = hi
        rhs[64:128, cols] = lo
        rhs[128:192, cols] = hi

    def mix(g):
        acc = None
        for q in range(Q):
            for d in range(3):
                term = jac[pl.ds(3 * g, 3), q, d:d + 1, :] * sp[d * B:(d + 1) * B, q * E:(q + 1) * E][None]
                acc = term if acc is None else acc + term
        return acc

    def face_mix(g, f, flow, trace, acc=None):
        for q in range(Q):
            term = flow[pl.ds(3 * g, 3), q, f:f + 1, :] * trace(q)[None]
            acc = term if acc is None else acc + term
        return acc

    def substep(j, carry):
        c = clus[0:1, :]
        length = jnp.where(c == 0, 1, jnp.where(c == 1, 2, 4)).astype(jnp.int32)
        lower = (jnp.bitwise_and(j, length - 1)).astype(F32) * STEP_LENGTH
        upper = lower + STEP_LENGTH
        low_power, up_power = lower, upper
        for k in range(ORDER):
            wt[k:k + 1, :] = (up_power - low_power) * ((-1.0) ** k / math.factorial(k + 1))
            low_power, up_power = low_power * lower, up_power * upper
        for q in range(Q):
            current = coef[q] + app[q]
            own[q] = current * wt[0:1, :]
            split_store(current, q)

        def degree(k, carry):
            sp[0:3 * B, :] = mm(w_d[...], rhs[...])
            weight = wt[pl.ds(k, 1), :]

            def group(g, carry):
                acc = mix(g)
                own[pl.ds(3 * g, 3)] = own[pl.ds(3 * g, 3)] + acc * weight[None]
                for i in range(3):
                    split_store(acc[i], 3 * g + i)
                return carry

            lax.fori_loop(0, 3, group, 0)
            return carry

        lax.fori_loop(1, ORDER, degree, 0)

        flat = jnp.concatenate([own[...].reshape(Q * B, E), jnp.zeros((8, E), F32)], axis=0)
        hi, lo = halves(flat)
        picked = lax.dot_general(oh_send[...], hi, NT, preferred_element_type=F32)
        picked = picked + lax.dot_general(oh_send[...], lo, NT, preferred_element_type=F32)
        for r in range(4):
            send[j, r] = picked[r * R:(r + 1) * R, :]

        @pl.when(j == 0)
        def _():
            pl.semaphore_wait(barrier, sum(jnp.where(h, 1, 0) for h in has))

        for r in (3, 2, 1, 0):
            @pl.when(has[r])
            def _():
                copy(j, r, OPPOSITE[r]).start()

        @pl.when(j == 0)
        def _():
            prepare_rest()

        for q in range(Q):
            split_store(own[q], q)
        sp[...] = mm(w_u[...], rhs[...])

        def local(g, carry):
            upd[pl.ds(3 * g, 3)] = mix(g)
            for f in range(4):
                rows = slice(3 * B + f * CP, 3 * B + (f + 1) * CP)
                flux[pl.ds(3 * g, 3), f * CP:(f + 1) * CP, :] = face_mix(
                    g, f, floc, lambda q: sp[rows, q * E:(q + 1) * E])
            return carry

        lax.fori_loop(0, 3, local, 0)
        tn[...] = mm(w_n[...], rhs[...])

        def turn(o, carry):
            rows = pl.ds(pl.multiple_of(o * CP, CP), CP)
            cols = pl.ds(pl.multiple_of(o * E, E), E)
            hi, lo = halves(jnp.concatenate([tn[rows, q * E:(q + 1) * E] for q in range(Q)], axis=0))
            tl_hi[:, cols] = hi
            tl_lo[:, cols] = lo
            return carry

        lax.fori_loop(0, ORIENTS, turn, 0)

        def near(n, carry):
            cols = pl.ds(pl.multiple_of(n * 256, 256), 256)
            trn[:, cols] = mm(tl_hi[...], oh_loc[:, cols]) + mm(tl_lo[...], oh_loc[:, cols])
            return carry

        lax.fori_loop(0, 2, near, 0)

        for r in range(4):
            @pl.when(has[r])
            def _():
                copy(j, r, r).wait_recv()

        got = recv[j].reshape(64, 512)
        tt[...] = jnp.concatenate([got, got], axis=0).T
        left = iota((B, E), 1) < 64
        for i in range(5):
            first = tt[2 * i * B:(2 * i + 1) * B, :]
            second = tt[(2 * i + 1) * B:(2 * i + 2) * B, :] if i < 4 else first
            x = jnp.where(left, first, second)
            hi, lo = halves(jnp.concatenate([x, jnp.zeros((64 - B, E), F32)], axis=0))
            cols = slice(i * E, (i + 1) * E)
            rhs_r[0:64, cols] = hi
            rhs_r[64:128, cols] = lo
            rhs_r[128:192, cols] = hi
        traces = mm(w_n[...], rhs_r[...])
        pair = jnp.broadcast_to(or_rem[0:1, :], (CP, E))
        parts = []
        for i in range(5):
            cols = slice(i * E, (i + 1) * E)
            chosen = traces[0:CP, cols]
            for o in range(1, ORIENTS):
                chosen = jnp.where(pair == float(o), traces[o * CP:(o + 1) * CP, cols], chosen)
            parts.append(chosen)
        hi, lo = halves(jnp.concatenate(parts, axis=0))
        far = mm(jnp.concatenate([hi, lo], axis=1), oh_rem[...])
        for q in range(Q):
            rows = slice(q * CP, (q + 1) * CP)
            trn[rows, :] = trn[rows, :] + far[
                (q // 2) * CP:(q // 2 + 1) * CP, (q % 2) * 512:(q % 2) * 512 + 512]

        def outer(g, carry):
            parts = []
            for f in range(4):
                parts.append(face_mix(
                    g, f, fnei, lambda q: trn[q * CP:(q + 1) * CP, f * E:(f + 1) * E],
                    flux[pl.ds(3 * g, 3), f * CP:(f + 1) * CP, :]))
            for i in range(3):
                hi, lo = halves(jnp.concatenate([part[i] for part in parts], axis=0))
                cols = pl.ds(pl.multiple_of((3 * g + i) * E, E), E)
                rhs_l[0:96, cols] = hi
                rhs_l[96:192, cols] = lo
                rhs_l[192:288, cols] = hi
            return carry

        lax.fori_loop(0, 3, outer, 0)
        lifted = mm(w_l[...], rhs_l[...])
        finished = jnp.broadcast_to(jnp.where(jnp.bitwise_and(j + 1, length - 1) == 0, 1.0, 0.0), (B, E)) > 0.5
        for p in range(Q):
            total = pend[p] + (upd[p] - lifted[:, p * E:(p + 1) * E])
            app[p] = app[p] + jnp.where(finished, total, 0.0)
            pend[p] = jnp.where(finished, 0.0, total)
        return carry

    lax.fori_loop(0, SUBSTEPS, substep, 0)
    out[...] = app[...]

    def drain(j, carry):
        for r in range(4):
            @pl.when(has[r])
            def _():
                copy(j, r, OPPOSITE[r]).wait_send()
        return carry

    lax.fori_loop(0, SUBSTEPS, drain, 0)


def on_device(coefficients, stiffness, jacobians, face_proj, neigh_proj, lifting, flux_local,
              flux_neigh, clusters, face_slots, orientation, send_list):
    vmem = pl.BlockSpec(memory_space=pltpu.VMEM)
    return pl.pallas_call(
        kernel,
        out_shape=jax.ShapeDtypeStruct((Q, B, E), F32),
        in_specs=[vmem] * 12,
        out_specs=vmem,
        scratch_shapes=[
            pltpu.VMEM((288, 192), F32),
            pltpu.VMEM((168, 192), BF16),
            pltpu.VMEM((264, 192), BF16),
            pltpu.VMEM((288, 192), BF16),
            pltpu.VMEM((B, 288), BF16),
            pltpu.VMEM((ORIENTS * E, 512), BF16),
            pltpu.VMEM((256, 1024), BF16),
            pltpu.VMEM((64, E), BF16),
            pltpu.VMEM((8, E), F32),
            pltpu.VMEM((192, Q * E), BF16),
            pltpu.VMEM((264, Q * E), F32),
            pltpu.VMEM((Q, B, E), F32),
            pltpu.VMEM((Q, B, E), F32),
            pltpu.VMEM((Q, B, E), F32),
            pltpu.VMEM((Q, B, E), F32),
            pltpu.VMEM((8, E), F32),
            pltpu.VMEM((Q * CP, 512), F32),
            pltpu.VMEM((288, Q * E), F32),
            pltpu.VMEM((Q * CP, ORIENTS * E), BF16),
            pltpu.VMEM((Q * CP, ORIENTS * E), BF16),
            pltpu.VMEM((Q, 96, E), F32),
            pltpu.VMEM((288, Q * E), BF16),
            pltpu.VMEM((192, 640), BF16),
            pltpu.VMEM((512, E), F32),
            pltpu.VMEM((SUBSTEPS, 4, R, 512), F32),
            pltpu.VMEM((SUBSTEPS, 4, R, 512), F32),
            pltpu.SemaphoreType.DMA((SUBSTEPS, 4)),
            pltpu.SemaphoreType.DMA((SUBSTEPS, 4)),
        ],
        compiler_params=pltpu.CompilerParams(collective_id=0, has_side_effects=True),
    )(coefficients, stiffness, jacobians.transpose(1, 2, 0, 3), face_proj.transpose(1, 0, 2), neigh_proj,
      lifting.transpose(2, 0, 1), flux_local.transpose(1, 2, 0, 3), flux_neigh.transpose(1, 2, 0, 3),
      clusters.reshape(1, E), face_slots, orientation, send_list)


def solution(mesh):
    placed = (
        P(None, None, ("dom", "sub")),
        P(),
        P(None, None, None, ("dom", "sub")),
        P(),
        P(),
        P(),
        P(None, None, None, ("dom", "sub")),
        P(None, None, None, ("dom", "sub")),
        P(("dom", "sub")),
        P(None, ("dom", "sub")),
        P(None, ("dom", "sub")),
        P(None, ("dom", "sub")),
    )
    return jax.shard_map(
        on_device,
        mesh=mesh,
        in_specs=placed,
        out_specs=P(None, None, ("dom", "sub")),
        check_vma=False,
    )
```

profile of v0, /device:TPU:60, one launch (start us, length us, event | category | flops | bytes accessed | tf_op | source)
XLA Modules:
  0.0 63.9 jit_solution(14108063975645797164)
XLA Ops:
  0.0 62.2 %shard_map.118 = f32[9,56,128]{2,1,0:T(8,128)} custom-call(f32[9,56,128]{2,1,0:T(8,128)} %coef.1, f32[3,56,56]{2,1,0:T(8,128)} %stiff.1, f32[9,9,3,128]{3,2,1,0:T(4,128)} %bitcast.6, f32[21,4,56]{2,1,0:T(4,128)} %bitcast.9, f32[12,21,56]{2,1,0:T(8,128)} %nproj.1, f32[21,4,56]{2,1,0:T(4,128)} %bitcast.10, f32[9,9,4,128]{3,2,1,0:T(4,128)} %bitcast.7, ...), custom_call_target="tpu_custom_call" | custom-call | tf_op jit(solution)/shard_map/pallas_call | solution.py:327
  62.2 1.7 %copy.14 = f32[9,56,128]{2,1,0:T(8,128)} copy(f32[9,56,128]{2,1,0:T(8,128)} %shard_map.118) | data formatting | bytes 516096
where the time goes:
time: 64.1 us; the launch traced here: 63.9 us
  Pallas kernels  62.2 us (97%)
  local copies, waits for them, and re-layouts  1.66 us (3%)
    pallas_call x1, Pallas kernels, on_device(): pl.pallas_call(kernel, out_shape=jax.ShapeDtypeStruct((Q, B, E), F32), in...  62.2 us
    unnamed x1, local copies, waits for them, and re-layouts  1.66 us

commit v1 on v0

--- a/solution.py
+++ b/solution.py
@@ -22,7 +22,6 @@
 MESH = pl.DeviceIdType.MESH
 OPPOSITE = (1, 0, 3, 2)
 NT = (((1,), (1,)), ((), ()))
-HIGHEST = lax.Precision.HIGHEST
 
 
 def iota(shape, dim):
@@ -36,10 +35,6 @@
 
 def mm(a, b):
     return jnp.dot(a, b, preferred_element_type=F32)
-
-
-def exact(a, b):
-    return jnp.dot(a, b, preferred_element_type=F32, precision=HIGHEST)
 
 
 def onehot(cond):
@@ -78,19 +73,25 @@
             device_id_type=MESH,
         )
 
-    def triple(rows, width, step, x):
-        place = jnp.where(
-            (iota((x.shape[1], width), 1) % step == iota((x.shape[1], width), 0))
-            & (iota((x.shape[1], width), 1) < 3 * step), 1.0, 0.0)
-        return exact(x, place)
-
-    def pack(x, step):
-        hi = x.astype(BF16).astype(F32)
-        return jnp.where(iota(x.shape, 1) < 2 * step, hi, x - hi).astype(BF16)
-
+    def spots(rows, width, step, low):
+        column, row = iota((rows, width), 1), iota((rows, width), 0)
+        part = (column >= 2 * step) & (column < 3 * step) if low else column < 2 * step
+        return onehot((column % step == row) & part)
+
+    def triple(x, at):
+        hi, lo = halves(x)
+        return mm(hi, at[0]) + mm(lo, at[1])
+
+    def turned(x, at, eye):
+        hi, lo = halves(x)
+        hi = lax.dot_general(eye, hi, NT, preferred_element_type=F32).astype(BF16)
+        lo = lax.dot_general(eye, lo, NT, preferred_element_type=F32).astype(BF16)
+        return mm(hi, at[0]) + mm(lo, at[1])
+
+    wide = (spots(B, 192, 64, False), spots(B, 192, 64, True))
     for d in range(3):
-        wf[d * B:(d + 1) * B, :] = triple(B, 192, 64, stiff[d])
-    w_d[...] = pack(wf[0:3 * B, :], 64)
+        wf[d * B:(d + 1) * B, :] = triple(stiff[d], wide)
+    w_d[...] = wf[0:3 * B, :].astype(BF16)
 
     def prepare_send():
         rows = iota((64, R), 0)
@@ -103,27 +104,25 @@
         oh_send[...] = onehot(iota((64, E), 1).astype(F32) == column)
 
     def prepare_rest():
-        eye = jnp.where(iota((B, B), 0) == iota((B, B), 1), 1.0, 0.0)
+        eye = onehot(iota((B, B), 0) == iota((B, B), 1))
+        wide = (spots(B, 192, 64, False), spots(B, 192, 64, True))
         for d in range(3):
-            turned = lax.dot_general(eye, stiff[d], NT, precision=HIGHEST, preferred_element_type=F32)
-            wf[d * B:(d + 1) * B, :] = triple(B, 192, 64, turned)
+            wf[d * B:(d + 1) * B, :] = turned(stiff[d], wide, eye)
         zero = jnp.zeros((CP - C, 192), F32)
         for f in range(4):
             wf[3 * B + f * CP:3 * B + (f + 1) * CP, :] = jnp.concatenate(
-                [triple(C, 192, 64, fproj[:, f, :]), zero], axis=0)
-        w_u[...] = pack(wf[0:3 * B + 4 * CP, :], 64)
+                [triple(fproj[:, f, :], wide), zero], axis=0)
+        w_u[...] = wf[0:3 * B + 4 * CP, :].astype(BF16)
         for o in range(ORIENTS):
-            wf[o * CP:(o + 1) * CP, :] = jnp.concatenate(
-                [triple(C, 192, 64, nproj[o]), zero], axis=0)
-        w_n[...] = pack(wf[...], 64)
+            wf[o * CP:(o + 1) * CP, :] = jnp.concatenate([triple(nproj[o], wide), zero], axis=0)
+        w_n[...] = wf[...].astype(BF16)
         total = None
         for f in range(4):
-            spot = iota((C, 288), 1)
-            place = jnp.where(spot % 96 == iota((C, 288), 0) + f * CP, 1.0, 0.0)
-            turned = lax.dot_general(eye, lift[:, f, :], NT, precision=HIGHEST, preferred_element_type=F32)
-            part = exact(turned, place)
+            column, row = iota((C, 288), 1), iota((C, 288), 0) + f * CP
+            at = (onehot((column % 96 == row) & (column < 192)), onehot((column % 96 == row) & (column >= 192)))
+            part = turned(lift[:, f, :], at, eye)
             total = part if total is None else total + part
-        w_l[...] = pack(total, 96)
+        w_l[...] = total.astype(BF16)
         for f in range(4):
             cols = slice(f * E, (f + 1) * E)
             row = jnp.broadcast_to(slots[f:f + 1, :], (E, E))
@@ -195,7 +194,7 @@
                     split_store(acc[i], 3 * g + i)
                 return carry
 
-            lax.fori_loop(0, 3, group, 0)
+            lax.fori_loop(0, 3, group, 0, unroll=True)
             return carry
 
         lax.fori_loop(1, ORDER, degree, 0)
@@ -226,13 +225,9 @@
 
         def local(g, carry):
             upd[pl.ds(3 * g, 3)] = mix(g)
-            for f in range(4):
-                rows = slice(3 * B + f * CP, 3 * B + (f + 1) * CP)
-                flux[pl.ds(3 * g, 3), f * CP:(f + 1) * CP, :] = face_mix(
-                    g, f, floc, lambda q: sp[rows, q * E:(q + 1) * E])
-            return carry
-
-        lax.fori_loop(0, 3, local, 0)
+            return carry
+
+        lax.fori_loop(0, 3, local, 0, unroll=True)
         tn[...] = mm(w_n[...], rhs[...])
 
         def turn(o, carry):
@@ -248,9 +243,17 @@
         def near(n, carry):
             cols = pl.ds(pl.multiple_of(n * 256, 256), 256)
             trn[:, cols] = mm(tl_hi[...], oh_loc[:, cols]) + mm(tl_lo[...], oh_loc[:, cols])
-            return carry
-
-        lax.fori_loop(0, 2, near, 0)
+            for i in range(2):
+                f = 2 * n + i
+                rows = pl.ds(pl.multiple_of(3 * B + f * CP, 8), CP)
+                acc = None
+                for q in range(Q):
+                    term = floc[:, q, pl.ds(f, 1), :] * sp[rows, q * E:(q + 1) * E][None]
+                    acc = term if acc is None else acc + term
+                flux[:, pl.ds(pl.multiple_of(f * CP, 8), CP), :] = acc
+            return carry
+
+        lax.fori_loop(0, 2, near, 0, unroll=True)
 
         for r in range(4):
             @pl.when(has[r])
@@ -299,7 +302,7 @@
                 rhs_l[192:288, cols] = hi
             return carry
 
-        lax.fori_loop(0, 3, outer, 0)
+        lax.fori_loop(0, 3, outer, 0, unroll=True)
         lifted = mm(w_l[...], rhs_l[...])
         finished = jnp.broadcast_to(jnp.where(jnp.bitwise_and(j + 1, length - 1) == 0, 1.0, 0.0), (B, E)) > 0.5
         for p in range(Q):

time: 64.1 us -> 61.5 us (0.959)
  Pallas kernels: 62.2 us -> 59.6 us
    pallas_call x1, Pallas kernels: 62.2 us -> 59.6 us  [on_device(): pl.pallas_call(kernel, out_shape=jax.ShapeDtypeStruct((Q, B, E), F32), in...]
where the time goes in v1:
time: 61.5 us; the launch traced here: 61.3 us
  Pallas kernels  59.6 us (97%)
  local copies, waits for them, and re-layouts  1.66 us (3%)
    pallas_call x1, Pallas kernels, on_device(): pl.pallas_call(kernel, out_shape=jax.ShapeDtypeStruct((Q, B, E), F32), in...  59.6 us
    unnamed x1, local copies, waits for them, and re-layouts  1.66 us

profile of v1, /device:TPU:60, one launch (start us, length us, event | category | flops | bytes accessed | tf_op | source)
XLA Modules:
  0.0 61.3 jit_solution(14324228320087015373)
XLA Ops:
  0.0 59.6 %shard_map.118 = f32[9,56,128]{2,1,0:T(8,128)} custom-call(f32[9,56,128]{2,1,0:T(8,128)} %coef.1, f32[3,56,56]{2,1,0:T(8,128)} %stiff.1, f32[9,9,3,128]{3,2,1,0:T(4,128)} %bitcast.6, f32[21,4,56]{2,1,0:T(4,128)} %bitcast.9, f32[12,21,56]{2,1,0:T(8,128)} %nproj.1, f32[21,4,56]{2,1,0:T(4,128)} %bitcast.10, f32[9,9,4,128]{3,2,1,0:T(4,128)} %bitcast.7, ...), custom_call_target="tpu_custom_call" | custom-call | tf_op jit(solution)/shard_map/pallas_call | solution.py:330
  59.6 1.7 %copy.14 = f32[9,56,128]{2,1,0:T(8,128)} copy(f32[9,56,128]{2,1,0:T(8,128)} %shard_map.118) | data formatting | bytes 516096
